TPU v7x, 32 devices: a whole 2x2x4 slice. The times are simulated.
32 devices in a mesh: seq: 16 (over z, y, x), head: 2 (over core).
Axes of the slice: x: 2, y: 2, z: 4, core: 2. Of those that a mesh axis runs over, the one named last changes fastest.
Arguments:
- queries: bfloat16 [4096, 4096], P('seq', 'head'), may hold values from -12 to 12
- key_input: bfloat16 [4096, 4096], P('seq', 'head'), may hold values from -1.796875 to 1.796875
- value_input: bfloat16 [4096, 4096], P('seq', 'head'), may hold values from -32 to 32
- norm_gain: bfloat16 [4096], P('head'), may hold values from 0.099609375 to 1.8984375
- out_weight: bfloat16 [4096, 3072], P('head', 'seq'), may hold values from -0.125 to 0.125
- target: bfloat16 [4096, 3072], P('seq', 'head'), may hold values from -6 to 6
Outputs:
- output: bfloat16 [4096, 3072], P('seq', 'head')
- query_grad: bfloat16 [4096, 4096], P('seq', 'head')
- key_grad: bfloat16 [4096, 4096], P('seq', 'head')
- value_grad: bfloat16 [4096, 4096], P('seq', 'head')
- gain_grads: float32 [16, 4096], P('seq', 'head')
- weight_grads: bfloat16 [16, 4096, 3072], P('seq', 'head')
All inputs are finite; a program needn't handle non-finite values.
Results may differ from a plain program's by a relative error of at most 0.022.
Values may be sent and summed in bfloat16 or wider, within the bound.
A program may use at most 128 MiB of HBM per device.

v0:
```python
import jax
import jax.numpy as jnp
from jax import lax
from jax.sharding import PartitionSpec as P

HEAD_DIM = 128
FEATURES = 4096
EPSILON = 1e-06


def entering(shard, axis, backward):
    count = lax.axis_size(axis)
    pieces = shard.astype(jnp.bfloat16).reshape(count, -1, shard.shape[-1])
    spread = lax.all_to_all(pieces, axis, 0, 0)
    row_index = lax.broadcasted_iota(jnp.int32, (count, count), 0)
    col_index = lax.broadcasted_iota(jnp.int32, (count, count), 1)
    chosen = col_index > row_index if backward else col_index < row_index
    sums = jnp.einsum(
        "ij,jrc->irc", chosen.astype(jnp.bfloat16), spread, preferred_element_type=jnp.float32
    )
    return lax.all_to_all(sums.astype(jnp.bfloat16), axis, 0, 0).reshape(shard.shape)


def causal(count):
    row_index = lax.broadcasted_iota(jnp.int32, (count, count), 0)
    col_index = lax.broadcasted_iota(jnp.int32, (count, count), 1)
    return row_index >= col_index


def per_device(queries, key_input, value_input, norm_gain, out_weight, target):
    tok_count = queries.shape[0]
    local_heads = queries.shape[1] // HEAD_DIM
    shape3 = (tok_count, local_heads, HEAD_DIM)
    q_heads = queries.reshape(shape3)
    k_heads = key_input.reshape(shape3)
    v_heads = value_input.reshape(shape3)
    keep_mask = causal(tok_count)
    f32 = jnp.float32
    state_local = jnp.einsum("shd,she->hde", k_heads, v_heads, preferred_element_type=f32)
    state_low = entering(state_local, "seq", False)
    scores = jnp.einsum("thd,shd->hts", q_heads, k_heads, preferred_element_type=f32)
    scores_low = jnp.where(keep_mask[None], scores, 0.0).astype(jnp.bfloat16)
    attended = jnp.einsum("hts,shd->thd", scores_low, v_heads, preferred_element_type=f32)
    attended = attended + jnp.einsum("thd,hde->the", q_heads, state_low, preferred_element_type=f32)
    mixed = attended.reshape(tok_count, -1)
    gain_float = norm_gain.astype(f32)
    squares = lax.psum(jnp.sum(mixed * mixed, axis=1, keepdims=True), "head")
    inverse = lax.rsqrt(squares / FEATURES + EPSILON)
    normed = (mixed * inverse * gain_float).astype(jnp.bfloat16)
    full_weight = lax.all_gather(out_weight, "seq", axis=1, tiled=True)
    partial_value = jnp.dot(normed, full_weight, preferred_element_type=f32)
    projected = lax.psum_scatter(
        partial_value.astype(jnp.bfloat16), "head", scatter_dimension=1, tiled=True
    ).astype(jnp.float32)
    output = projected.astype(jnp.bfloat16)
    grad_local = (projected - target.astype(f32)).astype(jnp.bfloat16)
    out_grad = lax.all_gather(grad_local, "head", axis=1, tiled=True)
    normed_grad = lax.dot_general(
        out_grad, full_weight, (((1,), (1,)), ((), ())), preferred_element_type=f32
    )
    product = jnp.sum(grad_local.astype(f32) * projected, axis=1, keepdims=True)
    inner = lax.psum(product, "head") / inverse
    mixed_grad = inverse * gain_float * normed_grad - mixed * inverse**3 * inner / FEATURES
    mixed_grad = mixed_grad.astype(jnp.bfloat16)
    gain_grads = jnp.sum(normed_grad * mixed * inverse, axis=0)[None]
    weight_grads = lax.dot_general(
        normed, out_grad, (((0,), (0,)), ((), ())), preferred_element_type=f32
    ).astype(jnp.bfloat16)[None]
    grad_heads = mixed_grad.reshape(shape3)
    grad_state = jnp.einsum("thd,the->hde", q_heads, grad_heads, preferred_element_type=f32)
    later_low = entering(grad_state, "seq", True)
    pairs = jnp.einsum("thd,shd->hts", grad_heads, v_heads, preferred_element_type=f32)
    pairs_low = jnp.where(keep_mask[None], pairs, 0.0).astype(jnp.bfloat16)
    query_grad = jnp.einsum("hts,shd->thd", pairs_low, k_heads, preferred_element_type=f32)
    query_grad = query_grad + jnp.einsum(
        "the,hde->thd", grad_heads, state_low, preferred_element_type=f32
    )
    key_grad = jnp.einsum("hts,thd->shd", pairs_low, q_heads, preferred_element_type=f32)
    key_grad = key_grad + jnp.einsum("she,hde->shd", v_heads, later_low, preferred_element_type=f32)
    value_grad = jnp.einsum("hts,the->she", scores_low, grad_heads, preferred_element_type=f32)
    value_grad = value_grad + jnp.einsum(
        "shd,hde->she", k_heads, later_low, preferred_element_type=f32
    )
    flat_shape = (tok_count, -1)
    return (
        output,
        query_grad.reshape(flat_shape).astype(jnp.bfloat16),
        key_grad.reshape(flat_shape).astype(jnp.bfloat16),
        value_grad.reshape(flat_shape).astype(jnp.bfloat16),
        gain_grads,
        weight_grads,
    )


def solution(mesh):
    placed = (
        P("seq", "head"),
        P("seq", "head"),
        P("seq", "head"),
        P("head"),
        P("head", "seq"),
        P("seq", "head"),
    )
    return jax.shard_map(
        per_device,
        mesh=mesh,
        in_specs=placed,
        out_specs=(
            P("seq", "head"),
            P("seq", "head"),
            P("seq", "head"),
            P("seq", "head"),
            P("seq", "head"),
            P("seq", "head", None),
        ),
        check_vma=False,
    )
```

profile of v0, /device:TPU:0, one launch (start us, length us, event | category | flops | bytes accessed | tf_op | source)
XLA Modules:
  0.0 288.4 jit_solution(15459992873029129070)
XLA Ops:
  7.9 2.5 copy.91
  12.5 30.5 %all_to_all.20 = bf16[16,128,128]{2,1,0:T(8,128)(2,1)S(1)} all-to-all(bf16[16,128,128]{2,1,0:T(8,128)(2,1)S(1)} %convolution_convert_fusion.4), channel_id=1, replica_groups=mesh['seq'=16,'head'=2] {'seq'}, dimensions={0} | all-to-all | bytes 1048576 | tf_op jit(solution)/shard_map/all_to_all | solution.py:14
  44.4 8.5 %all-to-all-start.1 = ((bf16[16,128,128]{2,1,0:T(8,128)(2,1)}), bf16[16,128,128]{2,1,0:T(8,128)(2,1)S(1)}, u32[]{:S(2)}, u32[]{:S(2)}) async-start(bf16[16,128,128]{2,1,0:T(8,128)(2,1)} %copy.62), calls=%async_computation.1 | async-start | bytes 1048576 | tf_op jit(solution)/shard_map/all_to_all | solution.py:21
  56.3 2.2 fusion.5
  58.4 14.0 %all-to-all-done.1 = bf16[16,128,128]{2,1,0:T(8,128)(2,1)S(1)} async-done(((bf16[16,128,128]{2,1,0:T(8,128)(2,1)}), bf16[16,128,128]{2,1,0:T(8,128)(2,1)S(1)}, u32[]{:S(2)}, u32[]{:S(2)}) %all-to-all-start.1) | async-done | bytes 524320 | tf_op jit(solution)/shard_map/all_to_all | solution.py:21
  72.4 3.6 %multiply_reduce_fusion.1 = (f32[256]{0:T(256)S(1)}, f32[256,16,128]{0,2,1:T(8,128)}) fusion(bf16[16,128,128]{2,1,0:T(8,128)(2,1)S(1)} %all-to-all-done.1, f32[16,256,128]{1,2,0:T(8,128)} %fusion.5, bf16[256,2048]{1,0:T(8,128)(2,1)S(1)} %copy-done), kind=kOutput, calls=%fused_computation.13 | convolution fusion | flops 135790336 | bytes 5768192 | tf_op jit(solution)/shard_map/thd,hde->the/dot_general | solution.py:44
  78.0 2.5 psum.14
  80.5 96.6 %all-gather.3.cloned.1.call-done = bf16[2048,3072]{0,1:T(8,128)(2,1)} async-done(((bf16[2048,192]{0,1:T(8,128)(2,1)}), bf16[2048,3072]{0,1:T(8,128)(2,1)}) %all-gather.3.cloned.1.call-update) | async-done | bytes 12582928 | tf_op jit(solution)/shard_map/all_gather | solution.py:50
  177.0 14.0 %convolution_convert_fusion = bf16[256,3072]{1,0:T(8,128)(2,1)} fusion(bf16[2048,3072]{0,1:T(8,128)(2,1)} %all-gather.3.cloned.1.call-done, f32[256,2048]{1,0:T(8,128)S(1)} %copy.65, f32[2048]{0:T(1024)S(1)} %convert_element_type.75, f32[256]{0:T(256)S(1)} %bitcast.127), kind=kOutput, calls=%fused_computation.3 | convolution fusion | flops 3223584768 | bytes 16262144 | tf_op jit(solution)/shard_map/dot_general | solution.py:51
  191.1 7.2 %reduce-scatter.2.cloned.1.call-done = bf16[256,1536]{1,0:T(8,128)(2,1)} async-done(((bf16[256,3072]{1,0:T(8,128)(2,1)}), bf16[256,1536]{1,0:T(8,128)(2,1)}) %reduce-scatter.2.cloned.1.call-update) | async-done | bytes 786448 | tf_op jit(solution)/shard_map/reduce_scatter | solution.py:52
  198.4 2.5 fusion.3
  200.9 2.7 psum.15
  203.6 8.6 %all-gather.5.cloned.1.call-done = bf16[256,3072]{1,0:T(8,128)(2,1)} async-done(((bf16[256,1536]{1,0:T(8,128)(2,1)}), bf16[256,3072]{1,0:T(8,128)(2,1)}) %all-gather.5.cloned.1.call-update) | async-done | bytes 1572880 | tf_op jit(solution)/shard_map/all_gather | solution.py:57
  212.2 10.4 %multiply_reduce_fusion = (f32[2048]{0:T(1024)}, bf16[256,2048]{1,0:T(8,128)(2,1)}) fusion(f32[256,2048]{1,0:T(8,128)S(1)} %copy.65, f32[256]{0:T(256)S(1)} %bitcast.128, f32[256]{0:T(256)S(1)} %bitcast.133, f32[256]{0:T(256)S(1)} %bitcast.132, f32[2048]{0:T(1024)S(1)} %convert_element_type.75, bf16[256,3072]{1,0:T(8,128)(2,1)} %all-gather.5.cloned.1.call-done, ...), kind=kOutput, calls=%fused_computation.9 | convolution fusion | flops 3226466304 | bytes 17320960 | tf_op jit(solution)/shard_map/dot_general | solution.py:58
  229.7 6.8 %all-to-all-start.2 = ((bf16[16,128,128]{2,1,0:T(8,128)(2,1)}), bf16[16,128,128]{2,1,0:T(8,128)(2,1)}, u32[]{:S(2)}, u32[]{:S(2)}) async-start(bf16[16,128,128]{2,1,0:T(8,128)(2,1)} %copy.74), calls=%async_computation.3 | async-start | bytes 1048576 | tf_op jit(solution)/shard_map/all_to_all | solution.py:14
  236.5 2.5 fusion.33
  240.9 3.4 %fusion.34 = f32[16,128,256]{2,1,0:T(8,128)} fusion(bf16[256,16,128]{0,2,1:T(8,128)(2,1)S(1)} %bitcast.120, bf16[16,256,256]{2,1,0:T(8,128)(2,1)} %copy-done.8), kind=kOutput, calls=%fused_computation.55 | convolution fusion | flops 268435456 | bytes 5242880 | tf_op jit(solution)/shard_map/hts,the->she/dot_general | solution.py:80
  244.3 7.8 %all-to-all-done.2 = bf16[16,128,128]{2,1,0:T(8,128)(2,1)} async-done(((bf16[16,128,128]{2,1,0:T(8,128)(2,1)}), bf16[16,128,128]{2,1,0:T(8,128)(2,1)}, u32[]{:S(2)}, u32[]{:S(2)}) %all-to-all-start.2) | async-done | bytes 524320 | tf_op jit(solution)/shard_map/all_to_all | solution.py:14
  254.4 4.2 %all-to-all-start.3 = ((bf16[16,128,128]{2,1,0:T(8,128)(2,1)}), bf16[16,128,128]{2,1,0:T(8,128)(2,1)}, u32[]{:S(2)}, u32[]{:S(2)}) async-start(bf16[16,128,128]{2,1,0:T(8,128)(2,1)} %copy.76), calls=%async_computation.4 | async-start | bytes 1048576 | tf_op jit(solution)/shard_map/all_to_all | solution.py:21
  261.5 6.7 %convert_bitcast_fusion = bf16[1,2048,3072]{2,1,0:T(8,128)(2,1)} fusion(bf16[256,3072]{1,0:T(8,128)(2,1)S(1)} %copy-done.13, f32[256,2048]{1,0:T(8,128)S(1)} %copy-done.2, f32[2048]{0:T(1024)S(1)} %convert_element_type.75, f32[256]{0:T(256)S(1)} %bitcast.129), kind=kOutput, calls=%fused_computation | convolution fusion | flops 3229089792 | bytes 16262144 | tf_op jit(solution)/shard_map/dot_general | solution.py:66
  268.2 4.8 %all-to-all-done.3 = bf16[16,128,128]{2,1,0:T(8,128)(2,1)} async-done(((bf16[16,128,128]{2,1,0:T(8,128)(2,1)}), bf16[16,128,128]{2,1,0:T(8,128)(2,1)}, u32[]{:S(2)}, u32[]{:S(2)}) %all-to-all-start.3) | async-done | bytes 524320 | tf_op jit(solution)/shard_map/all_to_all | solution.py:21
  273.0 2.9 add_convert_fusion
  275.9 2.4 copy.84
  278.2 2.2 fusion
  (56 shorter events, 25.0 us)
Async XLA Ops:
  7.2 45.9 %copy-start = (bf16[256,2048]{1,0:T(8,128)(2,1)S(1)}, bf16[256,2048]{1,0:T(8,128)(2,1)}, u32[]{:S(2)}) copy-start(bf16[256,2048]{1,0:T(8,128)(2,1)} %param.6) | copy-start | bytes 3145732
  7.2 169.8 %all-gather.3.cloned.1.call-start = ((), (), s32[]{:S(2)}) async-start(), calls=%async_computation.5 | async-start | bytes 13369344 | tf_op jit(solution)/shard_map/all_gather | solution.py:50
  7.9 4.2 %copy-start.5 = (bf16[256,2048]{1,0:T(8,128)(2,1)S(1)}, bf16[256,2048]{1,0:T(8,128)(2,1)}, u32[]{:S(2)}) copy-start(bf16[256,2048]{1,0:T(8,128)(2,1)} %param.8) | copy-start | bytes 3145732
  12.1 31.4 %copy-start.3 = (bf16[256,16,128]{0,2,1:T(8,128)(2,1)}, bf16[256,16,128]{0,2,1:T(8,128)(2,1)S(1)}, u32[]{:S(2)}) copy-start(bf16[256,16,128]{0,2,1:T(8,128)(2,1)S(1)} %copy.59) | copy-start | bytes 3145732
  12.5 40.4 %copy-start.14 = (bf16[2048]{0:T(1024)(128)(2,1)S(1)}, bf16[2048]{0:T(1024)(128)(2,1)}, u32[]{:S(2)}) copy-start(bf16[2048]{0:T(1024)(128)(2,1)} %param.9) | copy-start | bytes 12292
  44.4 28.0 %all-to-all-start.1 = ((bf16[16,128,128]{2,1,0:T(8,128)(2,1)}), bf16[16,128,128]{2,1,0:T(8,128)(2,1)S(1)}, u32[]{:S(2)}, u32[]{:S(2)}) async-start(bf16[16,128,128]{2,1,0:T(8,128)(2,1)} %copy.62), calls=%async_computation.1 | async-start | bytes 1048576 | tf_op jit(solution)/shard_map/all_to_all | solution.py:21
  52.9 145.5 %reduce-scatter.2.cloned.1.call-start = ((), (), s32[]{:S(2)}) async-start(), calls=%async_computation.6 | async-start | bytes 2359296 | tf_op jit(solution)/shard_map/reduce_scatter | solution.py:52
  55.0 1.3 copy-start.8
  72.4 3.6 %copy-start.11 = (bf16[16,128,128]{2,1,0:T(8,128)(2,1)}, bf16[16,128,128]{2,1,0:T(8,128)(2,1)S(1)}, u32[]{:S(2)}) copy-start(bf16[16,128,128]{2,1,0:T(8,128)(2,1)S(1)} %all-to-all-done.1) | copy-start | bytes 1572868
  78.0 134.2 %copy-start.1 = (f32[256,2048]{1,0:T(8,128)}, f32[256,2048]{1,0:T(8,128)S(1)}, u32[]{:S(2)}) copy-start(f32[256,2048]{1,0:T(8,128)S(1)} %copy.65) | copy-start | bytes 6291460
  191.1 21.1 %all-gather.5.cloned.1.call-start = ((), (), s32[]{:S(2)}) async-start(), calls=%async_computation.7 | async-start | bytes 2359296 | tf_op jit(solution)/shard_map/all_gather | solution.py:57
  222.6 2.8 copy-start.6
  227.5 9.0 %copy-start.4 = (bf16[256,16,128]{0,2,1:T(8,128)(2,1)S(1)}, bf16[256,16,128]{0,2,1:T(8,128)(2,1)}, u32[]{:S(2)}) copy-start(bf16[256,16,128]{0,2,1:T(8,128)(2,1)} %copy-done.3) | copy-start | bytes 3145732
  229.7 22.4 %all-to-all-start.2 = ((bf16[16,128,128]{2,1,0:T(8,128)(2,1)}), bf16[16,128,128]{2,1,0:T(8,128)(2,1)}, u32[]{:S(2)}, u32[]{:S(2)}) async-start(bf16[16,128,128]{2,1,0:T(8,128)(2,1)} %copy.74), calls=%async_computation.3 | async-start | bytes 1048576 | tf_op jit(solution)/shard_map/all_to_all | solution.py:14
  236.5 2.5 copy-start.12
  244.2 14.4 %copy-start.9 = (bf16[16,256,256]{2,1,0:T(8,128)(2,1)S(1)}, bf16[16,256,256]{2,1,0:T(8,128)(2,1)}, u32[]{:S(2)}) copy-start(bf16[16,256,256]{2,1,0:T(8,128)(2,1)} %select_convert_fusion) | copy-start | bytes 6291460
  254.4 18.6 %all-to-all-start.3 = ((bf16[16,128,128]{2,1,0:T(8,128)(2,1)}), bf16[16,128,128]{2,1,0:T(8,128)(2,1)}, u32[]{:S(2)}, u32[]{:S(2)}) async-start(bf16[16,128,128]{2,1,0:T(8,128)(2,1)} %copy.76), calls=%async_computation.4 | async-start | bytes 1048576 | tf_op jit(solution)/shard_map/all_to_all | solution.py:21
  258.7 1.9 copy-start.2
  258.7 2.8 copy-start.13
  261.5 11.5 %copy-start.10 = (f32[16,128,256]{2,1,0:T(8,128)S(1)}, f32[16,128,256]{2,1,0:T(8,128)}, u32[]{:S(2)}) copy-start(f32[16,128,256]{2,1,0:T(8,128)} %fusion.34) | copy-start | bytes 6291460
  275.9 2.4 copy-start.7
Sparse Core Ops, SparseCore 0:
  10.8 166.2 all-gather.2
  191.2 7.1 reduce-scatter.1
  201.0 11.0 all-gather.4
where the time goes:
time: 289 us; the launch traced here: 288 us
  waiting for transfers between devices  140 us (48%)
  matrix products  57.7 us (20%)
  blocking collectives  35.6 us (12%)
  starting transfers between devices  19.7 us (7%)
  local copies, waits for them, and re-layouts  19.1 us (7%)
  between operations  14 us (5%)
    all_gather x1, waiting for transfers between devices, per_device(): full_weight = lax.all_gather(out_weight, 'seq', axis=1, tiled=True)  96.6 us
    all_to_all x1, blocking collectives, entering(): spread = lax.all_to_all(pieces, axis, 0, 0)  30.5 us
    all_to_all x2, waiting for transfers between devices, entering(): lax.all_to_all(sums.astype(jnp.bfloat16), axis, 0, 0).reshape(shard.shape)  18.8 us
    dot_general x1, matrix products, per_device(): partial_value = jnp.dot(normed, full_weight, preferred_element_type=f32)  14 us
    all_to_all x2, starting transfers between devices, entering(): lax.all_to_all(sums.astype(jnp.bfloat16), axis, 0, 0).reshape(shard.shape)  12.7 us
    dot_general x1, matrix products, per_device(): lax.dot_general(out_grad, full_weight, (((1,), (1,)), ((), ())), preferre...  10.4 us
    unnamed x34, local copies, waits for them, and re-layouts  10 us
    all_gather x1, waiting for transfers between devices, per_device(): out_grad = lax.all_gather(grad_local, 'head', axis=1, tiled=True)  8.6 us
  transfers between devices with their start and end apart: 6, of which 6 were waited for; matrix products, arithmetic and copies ran while one was open for 11% of the time, Pallas kernels for 0%

commit v1 on v0

--- a/solution.py
+++ b/solution.py
@@ -47,7 +47,8 @@
     squares = lax.psum(jnp.sum(mixed * mixed, axis=1, keepdims=True), "head")
     inverse = lax.rsqrt(squares / FEATURES + EPSILON)
     normed = (mixed * inverse * gain_float).astype(jnp.bfloat16)
-    full_weight = lax.all_gather(out_weight, "seq", axis=1, tiled=True)
+    fit_sections = lambda content: jnp.concatenate(lax.all_gather(content, "seq"), axis=1)
+    full_weight = fit_sections(out_weight)
     partial_value = jnp.dot(normed, full_weight, preferred_element_type=f32)
     projected = lax.psum_scatter(
         partial_value.astype(jnp.bfloat16), "head", scatter_dimension=1, tiled=True

time: 289 us -> 321 us (1.11)
  local copies, waits for them, and re-layouts: 19.1 us -> 48 us
    reshape x0 -> x1, local copies, waits for them, and re-layouts: none -> 18.3 us  [per_device(): jnp.concatenate(lax.all_gather(content, 'seq'), axis=1)]
    unnamed x34 -> x31, local copies, waits for them, and re-layouts: 10 us -> 21.7 us
    all_gather x1, waiting for transfers between devices: 96.6 us -> 101 us  [per_device(): lax.all_gather(content, 'seq')]
  transfers between devices with their start and end apart: 6 -> 6, of which waited for: 6 -> 6; matrix products, arithmetic and copies ran while one was open for 11% -> 10% of each run, Pallas kernels for 0% -> 0%
where the time goes in v1:
time: 321 us; the launch traced here: 320 us
  waiting for transfers between devices  141 us (44%)
  matrix products  56.7 us (18%)
  local copies, waits for them, and re-layouts  48 us (15%)
  blocking collectives  35.8 us (11%)
  starting transfers between devices  19.9 us (6%)
  between operations  14 us (4%)
  other arithmetic  3.89 us (1%)
    all_gather x1, waiting for transfers between devices, per_device(): lax.all_gather(content, 'seq')  101 us
    all_to_all x1, blocking collectives, entering(): spread = lax.all_to_all(pieces, axis, 0, 0)  30.5 us
    unnamed x31, local copies, waits for them, and re-layouts  21.7 us
    all_to_all x2, waiting for transfers between devices, entering(): lax.all_to_all(sums.astype(jnp.bfloat16), axis, 0, 0).reshape(shard.shape)  19.3 us
    reshape x1, local copies, waits for them, and re-layouts, per_device(): jnp.concatenate(lax.all_gather(content, 'seq'), axis=1)  18.3 us
    dot_general x1, matrix products, per_device(): partial_value = jnp.dot(normed, full_weight, preferred_element_type=f32)  14 us
    all_to_all x2, starting transfers between devices, entering(): lax.all_to_all(sums.astype(jnp.bfloat16), axis, 0, 0).reshape(shard.shape)  13 us
    dot_general x1, matrix products, per_device(): lax.dot_general(out_grad, full_weight, (((1,), (1,)), ((), ())), preferre...  10 us
  transfers between devices with their start and end apart: 6, of which 6 were waited for; matrix products, arithmetic and copies ran while one was open for 10% of the time, Pallas kernels for 0%

profile of v1, /device:TPU:0, one launch (start us, length us, event | category | flops | bytes accessed | tf_op | source)
XLA Modules:
  0.0 319.9 jit_solution(15544852751830114839)
XLA Ops:
  7.9 2.5 copy.120
  12.5 30.5 %all_to_all.20 = bf16[16,128,128]{2,1,0:T(8,128)(2,1)S(1)} all-to-all(bf16[16,128,128]{2,1,0:T(8,128)(2,1)S(1)} %convolution_convert_fusion.4), channel_id=1, replica_groups=mesh['seq'=16,'head'=2] {'seq'}, dimensions={0} | all-to-all | bytes 1048576 | tf_op jit(solution)/shard_map/all_to_all | solution.py:14
  44.4 8.7 %all-to-all-start.1 = ((bf16[16,128,128]{2,1,0:T(8,128)(2,1)}), bf16[16,128,128]{2,1,0:T(8,128)(2,1)}, u32[]{:S(2)}, u32[]{:S(2)}) async-start(bf16[16,128,128]{2,1,0:T(8,128)(2,1)} %copy.91), calls=%async_computation.1 | async-start | bytes 1048576 | tf_op jit(solution)/shard_map/all_to_all | solution.py:21
  58.7 14.4 %all-to-all-done.1 = bf16[16,128,128]{2,1,0:T(8,128)(2,1)} async-done(((bf16[16,128,128]{2,1,0:T(8,128)(2,1)}), bf16[16,128,128]{2,1,0:T(8,128)(2,1)}, u32[]{:S(2)}, u32[]{:S(2)}) %all-to-all-start.1) | async-done | bytes 524320 | tf_op jit(solution)/shard_map/all_to_all | solution.py:21
  73.2 2.3 multiply_reduce_fusion.1
  75.5 2.7 psum.14
  79.4 100.7 %all-gather.6.cloned.1.call-done = bf16[32768,192]{0,1:T(8,128)(2,1)} async-done(((bf16[2048,192]{0,1:T(8,128)(2,1)}), bf16[32768,192]{0,1:T(8,128)(2,1)}) %all-gather.6.cloned.1.call-update) | async-done | bytes 12582928 | tf_op jit(solution)/shard_map/all_gather | solution.py:50
  180.2 11.7 %copy.121 = bf16[24,8,16,2048]{3,2,1,0:T(8,128)(2,1)S(1)} copy(bf16[24,8,16,2048]{3,1,2,0:T(8,128)(2,1)} %bitcast.135) | data formatting | bytes 25165824
  191.9 18.3 %copy.94 = bf16[2048,16,192]{0,2,1:T(8,128)(2,1)} copy(bf16[2048,16,192]{0,1,2:T(8,128)(2,1)S(1)} %bitcast.129) | data formatting | bytes 25165824 | tf_op jit(solution)/shard_map/reshape | solution.py:50
  210.1 14.0 %convolution_convert_fusion = bf16[256,3072]{1,0:T(8,128)(2,1)} fusion(bf16[256,2048]{0,1:T(8,128)(2,1)S(1)} %bitcast.143, bf16[2048,3072]{0,1:T(8,128)(2,1)} %bitcast.136), kind=kOutput, calls=%fused_computation.3 | convolution fusion | flops 3222011904 | bytes 15204352 | tf_op jit(solution)/shard_map/dot_general | solution.py:52
  224.2 7.2 %reduce-scatter.2.cloned.1.call-done = bf16[256,1536]{1,0:T(8,128)(2,1)} async-done(((bf16[256,3072]{1,0:T(8,128)(2,1)}), bf16[256,1536]{1,0:T(8,128)(2,1)}) %reduce-scatter.2.cloned.1.call-update) | async-done | bytes 786448 | tf_op jit(solution)/shard_map/reduce_scatter | solution.py:53
  231.4 2.5 fusion.3
  235.8 2.7 psum.15
  238.5 6.7 %all-gather.4.cloned.1.call-done = bf16[256,3072]{1,0:T(8,128)(2,1)} async-done(((bf16[256,1536]{1,0:T(8,128)(2,1)}), bf16[256,3072]{1,0:T(8,128)(2,1)}) %all-gather.4.cloned.1.call-update) | async-done | bytes 1572880 | tf_op jit(solution)/shard_map/all_gather | solution.py:58
  245.2 10.0 %multiply_reduce_fusion = (f32[2048]{0:T(1024)}, bf16[256,2048]{1,0:T(8,128)(2,1)S(1)}) fusion(f32[256,2048]{1,0:T(8,128)} %copy.95, f32[256]{0:T(256)S(1)} %bitcast.145, f32[256]{0:T(256)S(1)} %bitcast.150, f32[256]{0:T(256)S(1)} %bitcast.149, f32[2048]{0:T(1024)S(1)} %get-tuple-element.36, bf16[256,3072]{1,0:T(8,128)(2,1)} %all-gather.4.cloned.1.call-done, ...), kind=kOutput, calls=%fused_computation.10 | convolution fusion | flops 3226466304 | bytes 17320960 | tf_op jit(solution)/shard_map/dot_general | solution.py:59
  259.1 6.8 %all-to-all-start.2 = ((bf16[16,128,128]{1,2,0:T(8,128)(2,1)}), bf16[16,128,128]{1,2,0:T(8,128)(2,1)}, u32[]{:S(2)}, u32[]{:S(2)}) async-start(bf16[16,128,128]{1,2,0:T(8,128)(2,1)} %fusion.4), calls=%async_computation.3 | async-start | bytes 1048576 | tf_op jit(solution)/shard_map/all_to_all | solution.py:14
  265.9 2.4 fusion.35
  271.3 3.4 %fusion.36 = f32[16,128,256]{2,1,0:T(8,128)} fusion(bf16[256,16,128]{0,2,1:T(8,128)(2,1)S(1)} %bitcast.134, bf16[16,256,256]{2,1,0:T(8,128)(2,1)} %copy-done.7), kind=kOutput, calls=%fused_computation.59 | convolution fusion | flops 268435456 | bytes 5242880 | tf_op jit(solution)/shard_map/hts,the->she/dot_general | solution.py:81
  274.6 6.8 %all-to-all-done.2 = bf16[16,128,128]{1,2,0:T(8,128)(2,1)} async-done(((bf16[16,128,128]{1,2,0:T(8,128)(2,1)}), bf16[16,128,128]{1,2,0:T(8,128)(2,1)}, u32[]{:S(2)}, u32[]{:S(2)}) %all-to-all-start.2) | async-done | bytes 524320 | tf_op jit(solution)/shard_map/all_to_all | solution.py:14
  286.0 4.2 %all-to-all-start.3 = ((bf16[16,128,128]{2,1,0:T(8,128)(2,1)}), bf16[16,128,128]{2,1,0:T(8,128)(2,1)}, u32[]{:S(2)}, u32[]{:S(2)}) async-start(bf16[16,128,128]{2,1,0:T(8,128)(2,1)} %copy.104), calls=%async_computation.4 | async-start | bytes 1048576 | tf_op jit(solution)/shard_map/all_to_all | solution.py:21
  293.0 6.7 %convert_bitcast_fusion = bf16[1,2048,3072]{2,1,0:T(8,128)(2,1)} fusion(bf16[256,3072]{1,0:T(8,128)(2,1)S(1)} %copy-done.10, f32[256,2048]{1,0:T(8,128)S(1)} %copy-done.1, f32[2048]{0:T(1024)S(1)} %get-tuple-element.36, f32[256]{0:T(256)S(1)} %bitcast.146), kind=kOutput, calls=%fused_computation | convolution fusion | flops 3229089792 | bytes 16262144 | tf_op jit(solution)/shard_map/dot_general | solution.py:67
  299.7 4.8 %all-to-all-done.3 = bf16[16,128,128]{2,1,0:T(8,128)(2,1)} async-done(((bf16[16,128,128]{2,1,0:T(8,128)(2,1)}), bf16[16,128,128]{2,1,0:T(8,128)(2,1)}, u32[]{:S(2)}, u32[]{:S(2)}) %all-to-all-start.3) | async-done | bytes 524320 | tf_op jit(solution)/shard_map/all_to_all | solution.py:21
  304.5 2.8 add_convert_fusion
  307.4 2.4 copy.113
  (55 shorter events, 30.6 us)
Async XLA Ops:
  7.2 46.1 %copy-start = (bf16[256,2048]{1,0:T(8,128)(2,1)S(1)}, bf16[256,2048]{1,0:T(8,128)(2,1)}, u32[]{:S(2)}) copy-start(bf16[256,2048]{1,0:T(8,128)(2,1)} %param.6) | copy-start | bytes 3145732
  7.2 173.0 %all-gather.6.cloned.1.call-start = ((), (), s32[]{:S(2)}) async-start(), calls=%async_computation.7 | async-start | bytes 13369344 | tf_op jit(solution)/shard_map/all_gather | solution.py:50
  7.9 4.2 %copy-start.4 = (bf16[256,2048]{1,0:T(8,128)(2,1)S(1)}, bf16[256,2048]{1,0:T(8,128)(2,1)}, u32[]{:S(2)}) copy-start(bf16[256,2048]{1,0:T(8,128)(2,1)} %param.8) | copy-start | bytes 3145732
  12.1 31.4 %copy-start.2 = (bf16[256,16,128]{0,2,1:T(8,128)(2,1)}, bf16[256,16,128]{0,2,1:T(8,128)(2,1)S(1)}, u32[]{:S(2)}) copy-start(bf16[256,16,128]{0,2,1:T(8,128)(2,1)S(1)} %copy.88) | copy-start | bytes 3145732
  12.5 40.7 %copy-start.12 = (bf16[2048]{0:T(1024)(128)(2,1)S(1)}, bf16[2048]{0:T(1024)(128)(2,1)}, u32[]{:S(2)}) copy-start(bf16[2048]{0:T(1024)(128)(2,1)} %param.9) | copy-start | bytes 12292
  44.4 28.7 %all-to-all-start.1 = ((bf16[16,128,128]{2,1,0:T(8,128)(2,1)}), bf16[16,128,128]{2,1,0:T(8,128)(2,1)}, u32[]{:S(2)}, u32[]{:S(2)}) async-start(bf16[16,128,128]{2,1,0:T(8,128)(2,1)} %copy.91), calls=%async_computation.1 | async-start | bytes 1048576 | tf_op jit(solution)/shard_map/all_to_all | solution.py:21
  53.2 178.3 %reduce-scatter.2.cloned.1.call-start = ((), (), s32[]{:S(2)}) async-start(), calls=%async_computation.5 | async-start | bytes 2359296 | tf_op jit(solution)/shard_map/reduce_scatter | solution.py:53
  55.2 1.3 copy-start.7
  191.9 18.3 %copy-start.11 = (bf16[256,16,128]{0,2,1:T(8,128)(2,1)S(1)}, bf16[256,16,128]{0,2,1:T(8,128)(2,1)}, u32[]{:S(2)}) copy-start(bf16[256,16,128]{0,2,1:T(8,128)(2,1)} %multiply_convert_fusion.1) | copy-start | bytes 3145732
  224.2 21.1 %all-gather.4.cloned.1.call-start = ((), (), s32[]{:S(2)}) async-start(), calls=%async_computation.6 | async-start | bytes 2359296 | tf_op jit(solution)/shard_map/all_gather | solution.py:58
  255.7 1.2 copy-start.5
  257.0 9.0 %copy-start.3 = (bf16[256,16,128]{0,2,1:T(8,128)(2,1)S(1)}, bf16[256,16,128]{0,2,1:T(8,128)(2,1)}, u32[]{:S(2)}) copy-start(bf16[256,16,128]{0,2,1:T(8,128)(2,1)} %copy-done.2) | copy-start | bytes 3145732
  259.1 22.4 %all-to-all-start.2 = ((bf16[16,128,128]{1,2,0:T(8,128)(2,1)}), bf16[16,128,128]{1,2,0:T(8,128)(2,1)}, u32[]{:S(2)}, u32[]{:S(2)}) async-start(bf16[16,128,128]{1,2,0:T(8,128)(2,1)} %fusion.4), calls=%async_computation.3 | async-start | bytes 1048576 | tf_op jit(solution)/shard_map/all_to_all | solution.py:14
  274.6 15.6 %copy-start.8 = (bf16[16,256,256]{2,1,0:T(8,128)(2,1)S(1)}, bf16[16,256,256]{2,1,0:T(8,128)(2,1)}, u32[]{:S(2)}) copy-start(bf16[16,256,256]{2,1,0:T(8,128)(2,1)} %select_convert_fusion) | copy-start | bytes 6291460
  286.0 18.6 %all-to-all-start.3 = ((bf16[16,128,128]{2,1,0:T(8,128)(2,1)}), bf16[16,128,128]{2,1,0:T(8,128)(2,1)}, u32[]{:S(2)}, u32[]{:S(2)}) async-start(bf16[16,128,128]{2,1,0:T(8,128)(2,1)} %copy.104), calls=%async_computation.4 | async-start | bytes 1048576 | tf_op jit(solution)/shard_map/all_to_all | solution.py:21
  290.2 1.9 copy-start.1
  290.2 2.8 copy-start.10
  293.0 11.5 %copy-start.9 = (f32[16,128,256]{2,1,0:T(8,128)S(1)}, f32[16,128,256]{2,1,0:T(8,128)}, u32[]{:S(2)}) copy-start(f32[16,128,256]{2,1,0:T(8,128)} %fusion.36) | copy-start | bytes 6291460
  307.4 2.4 copy-start.6
Sparse Core Ops, SparseCore 0:
  10.7 169.3 all-gather.5
  224.3 7.0 reduce-scatter.1
  234.1 11.0 all-gather.3
